TPU v7x, 256 devices: a whole 4x4x8 slice. The times are simulated.
256 devices in a mesh: row: 8 (over z), col: 32 (over y, x, core).
Axes of the slice: x: 4, y: 4, z: 8, core: 2. Of those that a mesh axis runs over, the one named last changes fastest.
Arguments:
- inverse_first: float32 [512, 512], P('row'), may hold values from -0.4 to 2
- inverse_second: float32 [512, 512], P('row'), may hold values from -0.4 to 2
- coupling: float32 [512, 512], P('row'), may hold values from -0.25 to 0.25
- panel_first: float32 [32768, 512], P('row', 'col'), may hold values from -0.1875 to 0.1875
- panel_second: float32 [32768, 512], P('row', 'col'), may hold values from -0.1875 to 0.1875
- rhs_first: float32 [512, 8192], P('row', 'col'), may hold values from -6 to 6
- rhs_second: float32 [512, 8192], P('row', 'col'), may hold values from -6 to 6
- rhs_rest: float32 [32768, 8192], P('row', 'col'), may hold values from -6 to 6
Outputs:
- solved_first: float32 [512, 8192], P('row', 'col')
- solved_second: float32 [512, 8192], P('row', 'col')
- updated: float32 [32768, 8192], P('row', 'col')
All inputs are finite; a program needn't handle non-finite values.
Results may differ from a plain program's by a relative error of at most 0.00011.
Values sent between devices are 32-bit elements; how exact they have to be, the bound alone decides.
A program may use at most 64 MiB of HBM per device.

v0:
```python
import jax
import jax.numpy as jnp
from jax import lax
from jax.sharding import PartitionSpec as P


def product(left, right):
    return jnp.dot(left, right, precision=lax.Precision.HIGHEST, preferred_element_type=jnp.float32)


def per_device(
    inverse_first,
    inverse_second,
    coupling,
    panel_first,
    panel_second,
    rhs_first,
    rhs_second,
    rhs_rest,
):

    def apply_inverse(matrix, piece):
        return product(matrix, piece)

    solved_first = apply_inverse(
        inverse_first, lax.all_gather(rhs_first, "row", axis=0, tiled=True)
    )
    first_full = lax.all_gather(solved_first, "row", axis=0, tiled=True)
    reduced = rhs_second - product(coupling, first_full)
    solved_second = apply_inverse(
        inverse_second, lax.all_gather(reduced, "row", axis=0, tiled=True)
    )
    second_full = lax.all_gather(solved_second, "row", axis=0, tiled=True)
    updated = (
        rhs_rest
        - product(lax.all_gather(panel_first, "col", axis=1, tiled=True), first_full)
        - product(lax.all_gather(panel_second, "col", axis=1, tiled=True), second_full)
    )
    return (solved_first, solved_second, updated)


def solution(mesh):
    in_specs = (
        P("row", None),
        P("row", None),
        P("row", None),
        P("row", "col"),
        P("row", "col"),
        P("row", "col"),
        P("row", "col"),
        P("row", "col"),
    )
    out_specs = (P("row", "col"), P("row", "col"), P("row", "col"))
    return jax.shard_map(
        per_device, mesh=mesh, in_specs=in_specs, out_specs=out_specs, check_vma=False
    )
```

profile of v0, /device:TPU:1, one launch (start us, length us, event | category | flops | bytes accessed | tf_op | source)
XLA Modules:
  0.0 156.6 jit_solution(11201375104543490710)
XLA Ops:
  7.2 0.0 copy-start
  7.2 0.0 all-gather.3.cloned.1.call-start
  7.2 0.7 all-gather.3.cloned.1.call-update
  7.9 0.0 all-gather.5.cloned.1.call-start
  8.0 0.7 all-gather.5.cloned.1.call-update
  8.7 0.0 copy-start.5
  8.7 0.0 copy-start.3
  8.7 0.0 copy-start.6
  8.7 0.0 copy-start.4
  8.7 5.7 %copy.11 = f32[4096,256]{0,1:T(8,128)} copy(f32[4096,256]{1,0:T(8,128)} %param.15) | data formatting | bytes 8388608 | tf_op args[7]
  14.4 23.8 %all_gather.18 = f32[512,256]{1,0:T(8,128)S(1)} all-gather(f32[64,256]{1,0:T(8,128)S(1)} %copy-done.5), channel_id=1, replica_groups=mesh['row'=8,'col'=32] {'row'}, dimensions={0}, use_global_device_ids=true | all-gather | bytes 589824 | tf_op jit(solution)/shard_map/all_gather | solution.py:26
  38.2 0.4 fusion.3
  38.6 0.0 copy-start.1
  38.6 20.8 %all_gather.19 = f32[512,256]{1,0:T(8,128)S(1)} all-gather(f32[64,256]{1,0:T(8,128)S(1)} %fusion.3), channel_id=1, replica_groups=mesh['row'=8,'col'=32] {'row'}, dimensions={0}, use_global_device_ids=true | all-gather | bytes 589824 | tf_op jit(solution)/shard_map/all_gather | solution.py:28
  59.4 0.4 fusion.2
  59.8 20.8 %all_gather.20 = f32[512,256]{1,0:T(8,128)S(1)} all-gather(f32[64,256]{1,0:T(8,128)S(1)} %fusion.2), channel_id=1, replica_groups=mesh['row'=8,'col'=32] {'row'}, dimensions={0}, use_global_device_ids=true | all-gather | bytes 589824 | tf_op jit(solution)/shard_map/all_gather | solution.py:31
  80.6 0.4 convolution_bitcast_fusion.2
  81.1 0.0 copy-start.2
  81.1 19.9 %all_gather.22 = f32[512,256]{1,0:T(8,128)S(1)} all-gather(f32[64,256]{1,0:T(8,128)S(1)} %convolution_bitcast_fusion.2), channel_id=1, replica_groups=mesh['row'=8,'col'=32] {'row'}, dimensions={0}, use_global_device_ids=true | all-gather | bytes 589824 | tf_op jit(solution)/shard_map/all_gather | solution.py:33
  101.0 11.5 %fusion.1 = f32[4096,256]{0,1:T(8,128)} fusion(f32[4096,256]{0,1:T(8,128)} %copy.11, f32[512,256]{1,0:T(8,128)S(1)} %all_gather.19, f32[4096,512]{0,1:T(8,128)} %all-gather.3.cloned.1.call-done), kind=kOutput, calls=%fused_computation.3 | convolution fusion | flops 6443499520 | bytes 17301504 | tf_op jit(solution)/shard_map/dot_general | solution.py:8
  112.5 0.0 copy-done.1
  112.5 20.1 %all-gather.5.cloned.1.call-done = f32[4096,512]{0,1:T(8,128)} async-done(((f32[4096,16]{0,1:T(8,128)}), f32[4096,512]{0,1:T(8,128)}) %all-gather.5.cloned.1.call-update) | async-done | bytes 8388624 | tf_op jit(solution)/shard_map/all_gather | solution.py:37
  132.6 11.6 %fusion = f32[4096,256]{0,1:T(8,128)} fusion(f32[4096,256]{0,1:T(8,128)} %fusion.1, f32[512,256]{1,0:T(8,128)S(1)} %all_gather.22, f32[4096,512]{0,1:T(8,128)} %all-gather.5.cloned.1.call-done), kind=kOutput, calls=%fused_computation.1 | convolution fusion | flops 6443499520 | bytes 17301504 | tf_op jit(solution)/shard_map/dot_general | solution.py:8
  144.2 5.6 %copy.12 = f32[4096,256]{1,0:T(8,128)} copy(f32[4096,256]{0,1:T(8,128)} %fusion) | data formatting | bytes 8388608
  (7 shorter events, 0.0 us)
Async XLA Ops:
  7.2 31.0 %copy-start = (f32[64,512]{1,0:T(8,128)S(1)}, f32[64,512]{1,0:T(8,128)}, u32[]{:S(2)}) copy-start(f32[64,512]{1,0:T(8,128)} %param.8) | copy-start | bytes 393220
  7.2 93.8 %all-gather.3.cloned.1.call-start = ((), (), s32[]{:S(2)}) async-start(), calls=%async_computation | async-start | bytes 8650752 | tf_op jit(solution)/shard_map/all_gather | solution.py:36
  7.9 124.7 %all-gather.5.cloned.1.call-start = ((), (), s32[]{:S(2)}) async-start(), calls=%async_computation.1 | async-start | bytes 8650752 | tf_op jit(solution)/shard_map/all_gather | solution.py:37
  8.7 5.7 %copy-start.5 = (f32[64,256]{1,0:T(8,128)S(1)}, f32[64,256]{1,0:T(8,128)}, u32[]{:S(2)}) copy-start(f32[64,256]{1,0:T(8,128)} %param.13) | copy-start | bytes 196612
  8.7 50.7 %copy-start.3 = (f32[64,512]{1,0:T(8,128)S(1)}, f32[64,512]{1,0:T(8,128)}, u32[]{:S(2)}) copy-start(f32[64,512]{1,0:T(8,128)} %param.10) | copy-start | bytes 393220
  8.7 50.7 %copy-start.6 = (f32[64,256]{1,0:T(8,128)S(1)}, f32[64,256]{1,0:T(8,128)}, u32[]{:S(2)}) copy-start(f32[64,256]{1,0:T(8,128)} %param.14) | copy-start | bytes 196612
  8.7 71.9 %copy-start.4 = (f32[64,512]{1,0:T(8,128)S(1)}, f32[64,512]{1,0:T(8,128)}, u32[]{:S(2)}) copy-start(f32[64,512]{1,0:T(8,128)} %param.9) | copy-start | bytes 393220
  38.6 73.9 %copy-start.1 = (f32[64,256]{1,0:T(8,128)}, f32[64,256]{1,0:T(8,128)S(1)}, u32[]{:S(2)}) copy-start(f32[64,256]{1,0:T(8,128)S(1)} %fusion.3) | copy-start | bytes 196612
  81.1 31.4 %copy-start.2 = (f32[64,256]{1,0:T(8,128)}, f32[64,256]{1,0:T(8,128)S(1)}, u32[]{:S(2)}) copy-start(f32[64,256]{1,0:T(8,128)S(1)} %convolution_bitcast_fusion.2) | copy-start | bytes 196612
Sparse Core Ops, SparseCore 0:
  10.5 61.9 all-gather.2
  75.1 57.4 all-gather.4
where the time goes:
time: 158 us; the launch traced here: 157 us
  blocking collectives  85.3 us (54%)
  matrix products  24.4 us (15%)
  waiting for transfers between devices  21.5 us (14%)
  between operations  14.1 us (9%)
  local copies, waits for them, and re-layouts  11.3 us (7%)
    dot_general x5, matrix products, product(): jnp.dot(left, right, precision=lax.Precision.HIGHEST, preferred_element_t...  24.4 us
    all_gather x1, blocking collectives, per_device(): lax.all_gather(rhs_first, 'row', axis=0, tiled=True)  23.8 us
    all_gather x1, blocking collectives, per_device(): lax.all_gather(reduced, 'row', axis=0, tiled=True)  20.8 us
    all_gather x1, blocking collectives, per_device(): first_full = lax.all_gather(solved_first, 'row', axis=0, tiled=True)  20.8 us
    all_gather x1, waiting for transfers between devices, per_device(): lax.all_gather(panel_second, 'col', axis=1, tiled=True)  20.1 us
    all_gather x1, blocking collectives, per_device(): second_full = lax.all_gather(solved_second, 'row', axis=0, tiled=True)  19.9 us
    unnamed x16, local copies, waits for them, and re-layouts  11.3 us
  transfers between devices with their start and end apart: 2, of which 1 were waited for; matrix products, arithmetic and copies ran while one was open for 12% of the time, Pallas kernels for 0%

commit v1 on v0

v1 whole, which is shorter than its diff:
```python
import functools

import jax
import jax.numpy as jnp
from jax import lax
from jax.experimental import pallas as pl
from jax.experimental.pallas import tpu as pltpu
from jax.sharding import PartitionSpec as P

MESH = pl.DeviceIdType.MESH
NG = 8
AHEAD = 2


def split(v):
    hi = v.astype(jnp.bfloat16)
    return hi, (v - hi.astype(jnp.float32)).astype(jnp.bfloat16)


def dot3(a, b):
    f = functools.partial(jnp.dot, preferred_element_type=jnp.float32)
    return f(a[0], b[0]) + (f(a[0], b[1]) + f(a[1], b[0]))


def kernel(
    a1, a2, cp, pt0, pt1, r1, r2, rest,
    out1, out2, upd,
    grid, zb1, zb2, xb1, xb2, sol, st,
    rsem, ssem, lsem, zrsem, zssem, zlsem, bsem,
):
    rows = pt0.shape[1] // NG
    z = lax.axis_index("row")
    col = lax.axis_index("col")
    y, x, h = col // 8, (col // 2) % 4, col % 2
    oh = 1 - h

    def cid(yy, xx, hh):
        return (yy * 4 + xx) * 2 + hh

    xp = (z, cid(y, (x + 1) % 4, h))
    xm = (z, cid(y, (x + 3) % 4, h))
    yp = (z, cid((y + 1) % 4, x, h))
    ym = (z, cid((y + 3) % 4, x, h))
    zp = ((z + 1) % 8, col)
    zm = ((z + 7) % 8, col)
    sib = (z, cid(y, x, oh))

    def send(src, dst, s, r, dev):
        pltpu.make_async_remote_copy(
            src_ref=src, dst_ref=dst, send_sem=s, recv_sem=r,
            device_id=dev, device_id_type=MESH,
        ).start()

    def take(ref, sem):
        pltpu.make_async_copy(ref, ref, sem).wait()

    panels = (
        (pt0, x, y, xp, xm, yp, ym),
        (pt1, y, x, yp, ym, xp, xm),
    )

    def local_own(g, p):
        pt, a, b = panels[p][:3]
        src = pt.at[:, pl.ds(pl.multiple_of(g * rows, rows), rows)]
        return pltpu.make_async_copy(src, grid.at[g, p, h, b, a], lsem.at[g, p])

    def stage_a(g):
        for p in range(2):
            pt, a, b, ap, am, bp, bm = panels[p]
            src = pt.at[:, pl.ds(pl.multiple_of(g * rows, rows), rows)]
            dst = grid.at[g, p, h, b, a]
            s = ssem.at[g, p]
            send(src, dst, s, rsem.at[g, p, 0], ap)
            send(src, dst, s, rsem.at[g, p, 1], am)
            send(src, dst, s, rsem.at[g, p, 3], bp)
            send(src, dst, s, rsem.at[g, p, 4], bm)

    def stage_b(g):
        for p in range(2):
            pt, a, b, ap, am, bp, bm = panels[p]
            s = ssem.at[g, p]
            for k, da, to, half in ((0, 3, ap, 0), (1, 1, am, 8)):
                ai = (a + da) % 4
                ref = grid.at[g, p, h, b, ai]
                take(ref, rsem.at[g, p, k])
                part = grid.at[g, p, h, b, ai, pl.ds(half, 8)]
                send(part, part, s, rsem.at[g, p, 2], to)
                send(ref, ref, s, rsem.at[g, p, 3], bp)
                send(ref, ref, s, rsem.at[g, p, 4], bm)

    def stage_c(g):
        for p in range(2):
            pt, a, b, ap, am, bp, bm = panels[p]
            s = ssem.at[g, p]
            ref = grid.at[g, p, h, b, (a + 2) % 4]
            take(ref, rsem.at[g, p, 2])
            send(ref, ref, s, rsem.at[g, p, 3], bp)
            send(ref, ref, s, rsem.at[g, p, 4], bm)
            local_own(g, p).wait()
            ref = grid.at[g, p, h, b]
            send(ref, ref, bsem.at[g, p], rsem.at[g, p, 6], sib)

    def stage_d(g):
        for p in range(2):
            pt, a, b, ap, am, bp, bm = panels[p]
            s = ssem.at[g, p]
            for k, db, to, half in ((3, 3, bp, 0), (4, 1, bm, 2)):
                bi = (b + db) % 4
                ref = grid.at[g, p, h, bi]
                take(ref, rsem.at[g, p, k])
                part = grid.at[g, p, h, bi, pl.ds(half, 2)]
                send(part, part, s, rsem.at[g, p, 5], to)
                send(ref, ref, bsem.at[g, p], rsem.at[g, p, 6], sib)

    def stage_e(g):
        for p in range(2):
            b = panels[p][2]
            ref = grid.at[g, p, h, (b + 2) % 4]
            take(ref, rsem.at[g, p, 5])
            send(ref, ref, bsem.at[g, p], rsem.at[g, p, 6], sib)

    def stage_f(g):
        acc = None
        for p in range(2):
            take(grid.at[g, p, oh], rsem.at[g, p, 6])
        for p in range(2):
            m = split(grid[g, p].reshape(32 * 16, rows))
            t = dot3((st[p, 0], st[p, 1]), m)
            acc = t if acc is None else acc + t
        here = pl.ds(pl.multiple_of(g * rows, rows), rows)
        upd[here, :] = upd[here, :] - acc.T

    mcols = pl.ds(pl.multiple_of(h * 256, 256), 256)
    batches = (
        (zb1, (r1, a1.at[:, mcols])),
        (zb2, (r2, cp.at[:, mcols], a2.at[:, mcols])),
    )

    def z_own(bt):
        zb, items = batches[bt]
        for i, src in enumerate(items):
            dst = zb.at[z, i]
            send(src, dst, zssem.at[bt], zrsem.at[bt, 0], zp)
            send(src, dst, zssem.at[bt], zrsem.at[bt, 3], zm)

    def z_local(bt):
        zb, items = batches[bt]
        return [
            pltpu.make_async_copy(src, zb.at[z, i], zlsem.at[bt, i])
            for i, src in enumerate(items)
        ]

    def z_hop(bt, k):
        zb = batches[bt][0]
        for d, to, half, at in ((8 - k, zp, 0, 0), (k, zm, 32, 3)):
            zi = (z + d) % 8
            ref = zb.at[zi]
            take(ref, zrsem.at[bt, at + k - 1])
            if k < 3:
                send(ref, ref, zssem.at[bt], zrsem.at[bt, at + k], to)
            else:
                part = zb.at[zi, :, pl.ds(half, 32)]
                send(part, part, zssem.at[bt], zrsem.at[bt, 6], to)

    def z_last(bt):
        zb = batches[bt][0]
        take(zb.at[(z + 4) % 8], zrsem.at[bt, 6])
        for c in z_local(bt):
            c.wait()
        if bt == 0:
            send(zb1.at[:, pl.ds(1, 1)], xb1, zssem.at[2], zrsem.at[0, 7], sib)
        else:
            send(zb2.at[:, pl.ds(1, 2)], xb2, zssem.at[3], zrsem.at[1, 7], sib)

    def apply(own, other, load):
        here = split(load(h).reshape(256, 256))
        there = split(load(oh).reshape(256, 256))
        return dot3(split(own.reshape(512, 256)), here) + dot3(
            split(other.reshape(512, 256)), there
        )

    def keep(p, s):
        order = [
            (o // 4 % 4 * 4 + o % 4) * 2 + o // 16 if p == 0
            else (o % 4 * 4 + o // 4 % 4) * 2 + o // 16
            for o in range(32)
        ]
        perm = jnp.concatenate([s[c * 16:c * 16 + 16] for c in order], axis=0)
        hi, lo = split(perm.T)
        st[p, 0] = hi
        st[p, 1] = lo

    def solve_first():
        take(xb1, zrsem.at[0, 7])
        s = apply(
            zb1[:, 1], xb1[:, 0], lambda q: zb1[pl.ds(q * 4, 4), 0]
        )
        sol[0] = s.reshape(8, 64, 256)
        out1[...] = sol[0, z]
        keep(0, s)

    def solve_second():
        take(xb2, zrsem.at[1, 7])
        red = zb2[:, 0].reshape(512, 256) - apply(
            zb2[:, 1], xb2[:, 0], lambda q: sol[0, pl.ds(q * 4, 4)]
        )
        sol[1] = red.reshape(8, 64, 256)
        s = apply(
            zb2[:, 2], xb2[:, 1], lambda q: sol[1, pl.ds(q * 4, 4)]
        )
        sol[1] = s.reshape(8, 64, 256)
        out2[...] = sol[1, z]
        keep(1, s)

    barrier = pltpu.get_barrier_semaphore()
    near = (xp, xm, yp, ym, zp, zm, sib)
    for dev in near:
        pl.semaphore_signal(barrier, inc=1, device_id=dev, device_id_type=MESH)
    pl.semaphore_wait(barrier, len(near))

    stage_a(0)
    z_own(0)
    for g in range(1, AHEAD + 1):
        stage_a(g)
    z_own(1)

    @pl.loop(0, NG)
    def _(g):
        for p in range(2):
            local_own(g, p).start()

    for bt in range(2):
        for c in z_local(bt):
            c.start()
    rest_copy = pltpu.make_async_copy(rest, upd, zlsem.at[0, 2])
    rest_copy.start()

    zplan = {
        0: (lambda: z_hop(0, 1),),
        1: (lambda: z_hop(0, 2), lambda: z_hop(1, 1)),
        2: (lambda: z_hop(0, 3), lambda: z_hop(1, 2)),
        3: (lambda: z_last(0), lambda: z_hop(1, 3)),
        4: (solve_first, lambda: z_last(1)),
        5: (solve_second, rest_copy.wait),
    }
    first = 5

    @pl.loop(0, NG + first)
    def _(t):
        @pl.when(t + AHEAD + 1 < NG)
        def _():
            stage_a(t + AHEAD + 1)

        for lag, stage in enumerate((stage_b, stage_c, stage_d, stage_e)):
            @pl.when((t >= lag) & (t < NG + lag))
            def _(lag=lag, stage=stage):
                stage(t - lag)

        for k, jobs in zplan.items():
            @pl.when(t == k)
            def _(jobs=jobs):
                for job in jobs:
                    job()

        @pl.when(t >= first)
        def _():
            stage_f(t - first)

    @pl.loop(0, NG)
    def _(g):
        for p in range(2):
            take(upd.at[pl.ds(0, 15 * rows // 16)], ssem.at[g, p])
            take(grid.at[g, p, h], bsem.at[g, p])

    take(zb1.at[pl.ds(0, 7)], zssem.at[0])
    take(zb2.at[pl.ds(0, 7)], zssem.at[1])
    take(xb1, zssem.at[2])
    take(xb2, zssem.at[3])


def per_device(
    inverse_first,
    inverse_second,
    coupling,
    panel_first,
    panel_second,
    rhs_first,
    rhs_second,
    rhs_rest,
):
    rows = rhs_rest.shape[0]
    f32 = jnp.float32
    group = rows // NG
    any_spec = pl.BlockSpec(memory_space=pl.ANY)
    vmem_spec = pl.BlockSpec(memory_space=pltpu.VMEM)
    sem = pltpu.SemaphoreType.DMA
    return pl.pallas_call(
        kernel,
        out_shape=(
            jax.ShapeDtypeStruct((64, 256), f32),
            jax.ShapeDtypeStruct((64, 256), f32),
            jax.ShapeDtypeStruct((rows, 256), f32),
        ),
        in_specs=[any_spec] * 8,
        out_specs=(vmem_spec,) * 3,
        scratch_shapes=[
            pltpu.VMEM((NG, 2, 2, 4, 4, 16, group), f32),
            pltpu.VMEM((8, 2, 64, 256), f32),
            pltpu.VMEM((8, 3, 64, 256), f32),
            pltpu.VMEM((8, 1, 64, 256), f32),
            pltpu.VMEM((8, 2, 64, 256), f32),
            pltpu.VMEM((2, 8, 64, 256), f32),
            pltpu.VMEM((2, 2, 256, 512), jnp.bfloat16),
            sem((NG, 2, 7)),
            sem((NG, 2)),
            sem((NG, 2)),
            sem((2, 8)),
            sem((4,)),
            sem((2, 3)),
            sem((NG, 2)),
        ],
        compiler_params=pltpu.CompilerParams(
            collective_id=0, has_side_effects=True, vmem_limit_bytes=48 * 1024 * 1024
        ),
    )(
        inverse_first,
        inverse_second,
        coupling,
        panel_first.T,
        panel_second.T,
        rhs_first,
        rhs_second,
        rhs_rest,
    )


def solution(mesh):
    in_specs = (
        P("row", None),
        P("row", None),
        P("row", None),
        P("row", "col"),
        P("row", "col"),
        P("row", "col"),
        P("row", "col"),
        P("row", "col"),
    )
    out_specs = (P("row", "col"), P("row", "col"), P("row", "col"))
    return jax.shard_map(
        per_device, mesh=mesh, in_specs=in_specs, out_specs=out_specs, check_vma=False
    )
```

time: 158 us -> 76.4 us (0.48)
  blocking collectives: 85.3 us -> 0 us
  Pallas kernels: 0 us -> 65.7 us
  matrix products: 24.4 us -> 0 us
  waiting for transfers between devices: 21.5 us -> 0 us
  between operations: 14.1 us -> 0.66 us
  local copies, waits for them, and re-layouts: 11.3 us -> 9.56 us
    all_gather x4 -> x0, blocking collectives: 85.3 us -> none  [the longest x1 23.8 us: per_device(): lax.all_gather(rhs_first, 'row', axis=0, tiled=True)]
    pallas_call x0 -> x1, Pallas kernels: none -> 65.7 us  [per_device(): pl.pallas_call(kernel, out_shape=(jax.ShapeDtypeStruct((64, 256), f32), j...]
    dot_general x5 -> x0, matrix products: 24.4 us -> none  [product(): jnp.dot(left, right, precision=lax.Precision.HIGHEST, preferred_element_t...]
    all_gather x2 -> x0, waiting for transfers between devices: 20.1 us -> none  [the longest x1 20.1 us: per_device(): lax.all_gather(panel_second, 'col', axis=1, tiled=True)]
    unnamed x16 -> x17, local copies, waits for them, and re-layouts: 11.3 us -> 9.56 us
  transfers between devices with their start and end apart: 2 -> 0, of which waited for: 1 -> 0; matrix products, arithmetic and copies ran while one was open for 12% -> 0% of each run, Pallas kernels for 0% -> 0%
where the time goes in v1:
time: 76.4 us; the launch traced here: 75.9 us
  Pallas kernels  65.7 us (86%)
  local copies, waits for them, and re-layouts  9.56 us (13%)
    pallas_call x1, Pallas kernels, per_device(): pl.pallas_call(kernel, out_shape=(jax.ShapeDtypeStruct((64, 256), f32), j...  65.7 us
    unnamed x17, local copies, waits for them, and re-layouts  9.56 us

profile of v1, /device:TPU:1, one launch (start us, length us, event | category | flops | bytes accessed | tf_op | source)
XLA Modules:
  0.0 75.9 jit_solution(2492447895444975992)
XLA Ops:
  0.6 0.0 copy-start
  0.6 0.9 %copy-done = f32[4096,16]{0,1:T(8,128)S(1)} copy-done((f32[4096,16]{0,1:T(8,128)S(1)}, f32[4096,16]{0,1:T(8,128)}, u32[]{:S(2)}) %copy-start) | copy-done | bytes 262168
  1.6 0.0 copy-start.1
  1.6 0.9 %copy-done.1 = f32[4096,16]{0,1:T(8,128)S(1)} copy-done((f32[4096,16]{0,1:T(8,128)S(1)}, f32[4096,16]{0,1:T(8,128)}, u32[]{:S(2)}) %copy-start.1) | copy-done | bytes 262168
  2.5 0.0 copy-start.2
  2.5 0.9 %copy-done.2 = f32[64,512]{1,0:T(8,128)S(1)} copy-done((f32[64,512]{1,0:T(8,128)S(1)}, f32[64,512]{1,0:T(8,128)}, u32[]{:S(2)}) %copy-start.2) | copy-done | bytes 131096
  3.4 0.0 copy-start.3
  3.4 0.9 %copy-done.3 = f32[64,512]{1,0:T(8,128)S(1)} copy-done((f32[64,512]{1,0:T(8,128)S(1)}, f32[64,512]{1,0:T(8,128)}, u32[]{:S(2)}) %copy-start.3) | copy-done | bytes 131096
  4.3 0.0 copy-start.4
  4.3 0.9 %copy-done.4 = f32[64,512]{1,0:T(8,128)S(1)} copy-done((f32[64,512]{1,0:T(8,128)S(1)}, f32[64,512]{1,0:T(8,128)}, u32[]{:S(2)}) %copy-start.4) | copy-done | bytes 131096
  5.2 0.0 copy-start.5
  5.3 0.8 %copy-done.5 = f32[64,256]{1,0:T(8,128)S(1)} copy-done((f32[64,256]{1,0:T(8,128)S(1)}, f32[64,256]{1,0:T(8,128)}, u32[]{:S(2)}) %copy-start.5) | copy-done | bytes 65560
  6.1 0.0 copy-start.6
  6.1 0.8 %copy-done.6 = f32[64,256]{1,0:T(8,128)S(1)} copy-done((f32[64,256]{1,0:T(8,128)S(1)}, f32[64,256]{1,0:T(8,128)}, u32[]{:S(2)}) %copy-start.6) | copy-done | bytes 65560
  6.9 65.7 %shard_map.103 = (f32[64,256]{1,0:T(8,128)S(1)}, f32[64,256]{1,0:T(8,128)S(1)}, f32[4096,256]{1,0:T(8,128)S(1)}) custom-call(f32[64,512]{1,0:T(8,128)S(1)} %copy-done.2, f32[64,512]{1,0:T(8,128)S(1)} %copy-done.3, f32[64,512]{1,0:T(8,128)S(1)} %copy-done.4, f32[16,4096]{1,0:T(8,128)S(1)} %bitcast.2, f32[16,4096]{1,0:T(8,128)S(1)} %bitcast.3, ...), custom_call_target="tpu_custom_call" | custom-call | tf_op jit(solution)/shard_map/pallas_call | solution.py:297
  72.6 0.6 copy.14
  73.3 0.6 copy.15
  73.9 2.0 %copy.16 = f32[4096,256]{1,0:T(8,128)} copy(f32[4096,256]{1,0:T(8,128)S(1)} %get-tuple-element.8) | data formatting | bytes 8388608
Async XLA Ops:
  0.6 1.0 %copy-start = (f32[4096,16]{0,1:T(8,128)S(1)}, f32[4096,16]{0,1:T(8,128)}, u32[]{:S(2)}) copy-start(f32[4096,16]{0,1:T(8,128)} %param.11) | copy-start | bytes 786436
  1.6 0.9 %copy-start.1 = (f32[4096,16]{0,1:T(8,128)S(1)}, f32[4096,16]{0,1:T(8,128)}, u32[]{:S(2)}) copy-start(f32[4096,16]{0,1:T(8,128)} %param.12) | copy-start | bytes 786436
  2.5 0.9 %copy-start.2 = (f32[64,512]{1,0:T(8,128)S(1)}, f32[64,512]{1,0:T(8,128)}, u32[]{:S(2)}) copy-start(f32[64,512]{1,0:T(8,128)} %a1.1) | copy-start | bytes 393220
  3.4 0.9 %copy-start.3 = (f32[64,512]{1,0:T(8,128)S(1)}, f32[64,512]{1,0:T(8,128)}, u32[]{:S(2)}) copy-start(f32[64,512]{1,0:T(8,128)} %a2.1) | copy-start | bytes 393220
  4.3 0.9 %copy-start.4 = (f32[64,512]{1,0:T(8,128)S(1)}, f32[64,512]{1,0:T(8,128)}, u32[]{:S(2)}) copy-start(f32[64,512]{1,0:T(8,128)} %cp.1) | copy-start | bytes 393220
  5.2 0.8 %copy-start.5 = (f32[64,256]{1,0:T(8,128)S(1)}, f32[64,256]{1,0:T(8,128)}, u32[]{:S(2)}) copy-start(f32[64,256]{1,0:T(8,128)} %r1.1) | copy-start | bytes 196612
  6.1 0.8 %copy-start.6 = (f32[64,256]{1,0:T(8,128)S(1)}, f32[64,256]{1,0:T(8,128)}, u32[]{:S(2)}) copy-start(f32[64,256]{1,0:T(8,128)} %r2.1) | copy-start | bytes 196612

commit v2 on v1

--- a/solution.py
+++ b/solution.py
@@ -9,8 +9,26 @@
 
 MESH = pl.DeviceIdType.MESH
 NG = 8
-AHEAD = 2
-
+HEAD = (
+    ("a", 0), ("o", 0), ("o", 1), ("a", 1), ("a", 2), ("a", 3),
+    ("a", 4), ("a", 5), ("a", 6), ("a", 7), ("b", 0), ("b", 1),
+    ("b", 2), ("b", 3), ("z0", 1), ("z1", 1), ("z0", 2), ("c", 0),
+    ("b", 4), ("c", 1), ("b", 5), ("c", 2), ("b", 6), ("c", 3),
+    ("b", 7), ("z1", 2), ("z0", 3), ("d", 0), ("c", 4), ("d", 1),
+    ("c", 5), ("d", 2), ("c", 6), ("z1", 3), ("d", 3), ("c", 7),
+    ("l", 0), ("s", 0), ("e", 0), ("d", 4), ("l", 1), ("e", 1),
+    ("d", 5), ("e", 2), ("d", 6), ("s", 1),
+)
+TAIL = (
+    (),
+    (("e", 3), ("d", 7),),
+    (),
+    (("e", 4),),
+    (("e", 5),),
+    (("e", 6),),
+    (("e", 7),),
+    (),
+)
 
 def split(v):
     hi = v.astype(jnp.bfloat16)
@@ -22,10 +40,37 @@
     return f(a[0], b[0]) + (f(a[0], b[1]) + f(a[1], b[0]))
 
 
+def panel_product(grid, st, g):
+    acc = None
+    for p in range(2):
+        m = split(grid[g, p].reshape(32 * 16, grid.shape[-1]))
+        t = dot3((st[p, 0], st[p, 1]), m)
+        acc = t if acc is None else acc + t
+    return acc
+
+
+def finish(out1, out2, upd, grid, st, o1, o2, o3, tail, sem):
+    rows = grid.shape[-1]
+    done = (NG - 1) * rows
+    copies = [
+        pltpu.make_async_copy(upd.at[pl.ds(0, done)], o3.at[pl.ds(0, done)], sem.at[0]),
+        pltpu.make_async_copy(out1, o1, sem.at[1]),
+        pltpu.make_async_copy(out2, o2, sem.at[2]),
+    ]
+    for c in copies:
+        c.start()
+    tail[...] = upd[pl.ds(done, rows), :] - panel_product(grid, st, NG - 1).T
+    last = pltpu.make_async_copy(tail, o3.at[pl.ds(done, rows)], sem.at[3])
+    last.start()
+    for c in copies:
+        c.wait()
+    last.wait()
+
+
 def kernel(
     a1, a2, cp, pt0, pt1, r1, r2, rest,
-    out1, out2, upd,
-    grid, zb1, zb2, xb1, xb2, sol, st,
+    out1, out2, upd, grid, st,
+    zb1, zb2, xb1, xb2, sol,
     rsem, ssem, lsem, zrsem, zssem, zlsem, bsem,
 ):
     rows = pt0.shape[1] // NG
@@ -120,15 +165,10 @@
             send(ref, ref, bsem.at[g, p], rsem.at[g, p, 6], sib)
 
     def stage_f(g):
-        acc = None
         for p in range(2):
             take(grid.at[g, p, oh], rsem.at[g, p, 6])
-        for p in range(2):
-            m = split(grid[g, p].reshape(32 * 16, rows))
-            t = dot3((st[p, 0], st[p, 1]), m)
-            acc = t if acc is None else acc + t
         here = pl.ds(pl.multiple_of(g * rows, rows), rows)
-        upd[here, :] = upd[here, :] - acc.T
+        upd[here, :] = upd[here, :] - panel_product(grid, st, g).T
 
     mcols = pl.ds(pl.multiple_of(h * 256, 256), 256)
     batches = (
@@ -218,53 +258,55 @@
         pl.semaphore_signal(barrier, inc=1, device_id=dev, device_id_type=MESH)
     pl.semaphore_wait(barrier, len(near))
 
-    stage_a(0)
-    z_own(0)
-    for g in range(1, AHEAD + 1):
-        stage_a(g)
-    z_own(1)
-
-    @pl.loop(0, NG)
+    stages = {
+        "a": stage_a,
+        "b": stage_b,
+        "c": stage_c,
+        "d": stage_d,
+        "e": stage_e,
+        "o": z_own,
+        "l": z_last,
+        "s": lambda bt: (solve_first, solve_second)[bt](),
+        "z0": lambda k: z_hop(0, k),
+        "z1": lambda k: z_hop(1, k),
+    }
+
+    def run(steps):
+        for name, arg in steps:
+            stages[name](arg)
+
+    def local_starts():
+        @pl.loop(0, NG)
+        def _(g):
+            for p in range(2):
+                local_own(g, p).start()
+
+        for bt in range(2):
+            for c in z_local(bt):
+                c.start()
+        rest_copy.start()
+
+    rest_copy = pltpu.make_async_copy(rest, upd, zlsem.at[0, 2])
+    count = sum(name in ("a", "o") for name, _ in HEAD)
+    run(HEAD[:count])
+    local_starts()
+    run(HEAD[count:])
+    rest_copy.wait()
+
+    @pl.loop(0, NG - 1)
     def _(g):
-        for p in range(2):
-            local_own(g, p).start()
-
-    for bt in range(2):
-        for c in z_local(bt):
-            c.start()
-    rest_copy = pltpu.make_async_copy(rest, upd, zlsem.at[0, 2])
-    rest_copy.start()
-
-    zplan = {
-        0: (lambda: z_hop(0, 1),),
-        1: (lambda: z_hop(0, 2), lambda: z_hop(1, 1)),
-        2: (lambda: z_hop(0, 3), lambda: z_hop(1, 2)),
-        3: (lambda: z_last(0), lambda: z_hop(1, 3)),
-        4: (solve_first, lambda: z_last(1)),
-        5: (solve_second, rest_copy.wait),
-    }
-    first = 5
-
-    @pl.loop(0, NG + first)
-    def _(t):
-        @pl.when(t + AHEAD + 1 < NG)
-        def _():
-            stage_a(t + AHEAD + 1)
-
-        for lag, stage in enumerate((stage_b, stage_c, stage_d, stage_e)):
-            @pl.when((t >= lag) & (t < NG + lag))
-            def _(lag=lag, stage=stage):
-                stage(t - lag)
-
-        for k, jobs in zplan.items():
-            @pl.when(t == k)
-            def _(jobs=jobs):
-                for job in jobs:
-                    job()
-
-        @pl.when(t >= first)
-        def _():
-            stage_f(t - first)
+        for k in range(NG - 1):
+            if TAIL[k]:
+                @pl.when(g == k)
+                def _(k=k):
+                    run(TAIL[k])
+
+        stage_f(g)
+
+    run(TAIL[NG - 1])
+
+    for p in range(2):
+        take(grid.at[NG - 1, p, oh], rsem.at[NG - 1, p, 6])
 
     @pl.loop(0, NG)
     def _(g):
@@ -291,26 +333,26 @@
     rows = rhs_rest.shape[0]
     f32 = jnp.float32
     group = rows // NG
-    any_spec = pl.BlockSpec(memory_space=pl.ANY)
+    any_spec = pl.BlockSpec(memory_space=pltpu.HBM)
     vmem_spec = pl.BlockSpec(memory_space=pltpu.VMEM)
     sem = pltpu.SemaphoreType.DMA
-    return pl.pallas_call(
+    mid = pl.pallas_call(
         kernel,
         out_shape=(
-            jax.ShapeDtypeStruct((64, 256), f32),
-            jax.ShapeDtypeStruct((64, 256), f32),
-            jax.ShapeDtypeStruct((rows, 256), f32),
+            pltpu.VMEM((64, 256), f32),
+            pltpu.VMEM((64, 256), f32),
+            pltpu.VMEM((rows, 256), f32),
+            pltpu.VMEM((NG, 2, 2, 4, 4, 16, group), f32),
+            pltpu.VMEM((2, 2, 256, 512), jnp.bfloat16),
         ),
         in_specs=[any_spec] * 8,
-        out_specs=(vmem_spec,) * 3,
+        out_specs=(vmem_spec,) * 5,
         scratch_shapes=[
-            pltpu.VMEM((NG, 2, 2, 4, 4, 16, group), f32),
             pltpu.VMEM((8, 2, 64, 256), f32),
             pltpu.VMEM((8, 3, 64, 256), f32),
             pltpu.VMEM((8, 1, 64, 256), f32),
             pltpu.VMEM((8, 2, 64, 256), f32),
             pltpu.VMEM((2, 8, 64, 256), f32),
-            pltpu.VMEM((2, 2, 256, 512), jnp.bfloat16),
             sem((NG, 2, 7)),
             sem((NG, 2)),
             sem((NG, 2)),
@@ -320,18 +362,35 @@
             sem((NG, 2)),
         ],
         compiler_params=pltpu.CompilerParams(
-            collective_id=0, has_side_effects=True, vmem_limit_bytes=48 * 1024 * 1024
+            collective_id=0, has_side_effects=True, vmem_limit_bytes=24 * 1024 * 1024
         ),
     )(
-        inverse_first,
-        inverse_second,
-        coupling,
-        panel_first.T,
-        panel_second.T,
-        rhs_first,
-        rhs_second,
-        rhs_rest,
+        *(
+            pltpu.with_memory_space_constraint(v, pltpu.HBM)
+            for v in (
+                inverse_first,
+                inverse_second,
+                coupling,
+                panel_first.T,
+                panel_second.T,
+                rhs_first,
+                rhs_second,
+                rhs_rest,
+            )
+        )
     )
+    return pl.pallas_call(
+        finish,
+        out_shape=(
+            jax.ShapeDtypeStruct((64, 256), f32),
+            jax.ShapeDtypeStruct((64, 256), f32),
+            jax.ShapeDtypeStruct((rows, 256), f32),
+        ),
+        in_specs=[vmem_spec] * 5,
+        out_specs=(any_spec,) * 3,
+        scratch_shapes=[pltpu.VMEM((group, 256), f32), sem((4,))],
+        compiler_params=pltpu.CompilerParams(vmem_limit_bytes=16 * 1024 * 1024),
+    )(*mid)
 
 
 def solution(mesh):

time: 76.4 us -> 61.4 us (0.80)
  local copies, waits for them, and re-layouts: 9.56 us -> 0 us
  Pallas kernels: 65.7 us -> 60.6 us
    unnamed x17 -> x0, local copies, waits for them, and re-layouts: 9.56 us -> none
    pallas_call x1 -> x2, Pallas kernels: 65.7 us -> 60.6 us  [the longest x1 58.6 us: per_device(): pl.pallas_call(kernel, out_shape=(pltpu.VMEM((64, 256), f32), pltpu.VMEM(...]
where the time goes in v2:
time: 61.4 us; the launch traced here: 61.3 us
  Pallas kernels  60.6 us (99%)
  between operations  0.64 us (1%)
    pallas_call x1, Pallas kernels, per_device(): pl.pallas_call(kernel, out_shape=(pltpu.VMEM((64, 256), f32), pltpu.VMEM(...  58.6 us
    pallas_call x1, Pallas kernels, per_device(): pl.pallas_call(finish, out_shape=(jax.ShapeDtypeStruct((64, 256), f32), j...  2.08 us

profile of v2, /device:TPU:1, one launch (start us, length us, event | category | flops | bytes accessed | tf_op | source)
XLA Modules:
  0.0 61.3 jit_solution(4325426153166046213)
XLA Ops:
  0.6 58.6 %shard_map.103 = (f32[64,256]{1,0:T(8,128)S(1)}, f32[64,256]{1,0:T(8,128)S(1)}, f32[4096,256]{1,0:T(8,128)S(1)}, f32[8,2,2,4,4,16,512]{6,5,4,3,2,1,0:T(8,128)S(1)}, bf16[2,2,256,512]{3,2,1,0:T(8,128)(2,1)S(1)}) custom-call(f32[64,512]{1,0:T(8,128)} %a1.1, f32[64,512]{1,0:T(8,128)} %a2.1, f32[64,512]{1,0:T(8,128)} %cp.1, f32[16,4096]{1,0:T(8,128)} %bitcast.2, ...), custom_call_target="tpu_custom_call" | custom-call | tf_op jit(solution)/shard_map/pallas_call | solution.py:339
  59.2 2.1 %shard_map.104 = (f32[64,256]{1,0:T(8,128)}, f32[64,256]{1,0:T(8,128)}, f32[4096,256]{1,0:T(8,128)}) custom-call(f32[64,256]{1,0:T(8,128)S(1)} %get-tuple-element.8.out1, f32[64,256]{1,0:T(8,128)S(1)} %get-tuple-element.9.out2, f32[4096,256]{1,0:T(8,128)S(1)} %get-tuple-element.10.upd, f32[8,2,2,4,4,16,512]{6,5,4,3,2,1,0:T(8,128)S(1)} %get-tuple-element.11.grid, ...), custom_call_target="tpu_custom_call" | custom-call | tf_op jit(solution)/shard_map/pallas_call | solution.py:382

commit v3 on v2

--- a/solution.py
+++ b/solution.py
@@ -10,19 +10,19 @@
 MESH = pl.DeviceIdType.MESH
 NG = 8
 HEAD = (
-    ("a", 0), ("o", 0), ("o", 1), ("a", 1), ("a", 2), ("a", 3),
-    ("a", 4), ("a", 5), ("a", 6), ("a", 7), ("b", 0), ("b", 1),
-    ("b", 2), ("b", 3), ("z0", 1), ("z1", 1), ("z0", 2), ("c", 0),
-    ("b", 4), ("c", 1), ("b", 5), ("c", 2), ("b", 6), ("c", 3),
-    ("b", 7), ("z1", 2), ("z0", 3), ("d", 0), ("c", 4), ("d", 1),
-    ("c", 5), ("d", 2), ("c", 6), ("z1", 3), ("d", 3), ("c", 7),
-    ("l", 0), ("s", 0), ("e", 0), ("d", 4), ("l", 1), ("e", 1),
-    ("d", 5), ("e", 2), ("d", 6), ("s", 1),
+    ("a", 0), ("a", 1), ("o", 0), ("a", 2), ("a", 3), ("o", 1),
+    ("a", 4), ("b", 0), ("a", 5), ("b", 1), ("b", 2), ("a", 6),
+    ("z0", 1), ("z1", 1), ("a", 7), ("c", 0), ("b", 3), ("b", 4),
+    ("c", 1), ("z0", 2), ("c", 2), ("b", 5), ("z1", 2), ("b", 6),
+    ("b", 7), ("z0", 3), ("c", 3), ("d", 0), ("c", 4), ("d", 1),
+    ("z1", 3), ("c", 5), ("c", 6), ("d", 2), ("l", 0), ("c", 7),
+    ("d", 3), ("l", 1), ("d", 4), ("e", 0), ("d", 5), ("s", 0),
+    ("e", 1), ("s", 1), ("d", 6),
 )
 TAIL = (
     (),
-    (("e", 3), ("d", 7),),
-    (),
+    (("e", 2), ("d", 7),),
+    (("e", 3),),
     (("e", 4),),
     (("e", 5),),
     (("e", 6),),
@@ -71,7 +71,7 @@
     a1, a2, cp, pt0, pt1, r1, r2, rest,
     out1, out2, upd, grid, st,
     zb1, zb2, xb1, xb2, sol,
-    rsem, ssem, lsem, zrsem, zssem, zlsem, bsem,
+    rsem, ssem, lsem, zrsem, zssem, zlsem, bsem, ready,
 ):
     rows = pt0.shape[1] // NG
     z = lax.axis_index("row")
@@ -252,11 +252,42 @@
         out2[...] = sol[1, z]
         keep(1, s)
 
+    def tell(sem, dev):
+        pl.semaphore_signal(sem, inc=1, device_id=dev, device_id_type=MESH)
+
     barrier = pltpu.get_barrier_semaphore()
-    near = (xp, xm, yp, ym, zp, zm, sib)
-    for dev in near:
-        pl.semaphore_signal(barrier, inc=1, device_id=dev, device_id_type=MESH)
-    pl.semaphore_wait(barrier, len(near))
+    for yy, xx in ((y, x + 1), (y, x + 3), (y + 1, x), (y + 3, x)):
+        tell(barrier, (z, cid(yy % 4, xx % 4, 0)))
+    for zz in (z + 1, z + 7):
+        tell(barrier, (zz % 8, cid(y, x, 1)))
+
+    @pl.when(h == 1)
+    def _():
+        tell(barrier, sib)
+
+    @pl.when(h == 0)
+    def _():
+        pl.semaphore_wait(barrier, 9)
+        tell(ready, sib)
+
+    @pl.when(h == 1)
+    def _():
+        pl.semaphore_wait(ready, 1)
+
+    def z_ready():
+        @pl.when(h == 1)
+        def _():
+            pl.semaphore_wait(barrier, 4)
+            tell(ready, sib)
+
+        @pl.when(h == 0)
+        def _():
+            pl.semaphore_wait(ready, 1)
+
+    def z_first(bt):
+        if bt == 0:
+            z_ready()
+        z_own(bt)
 
     stages = {
         "a": stage_a,
@@ -264,7 +295,7 @@
         "c": stage_c,
         "d": stage_d,
         "e": stage_e,
-        "o": z_own,
+        "o": z_first,
         "l": z_last,
         "s": lambda bt: (solve_first, solve_second)[bt](),
         "z0": lambda k: z_hop(0, k),
@@ -287,10 +318,9 @@
         rest_copy.start()
 
     rest_copy = pltpu.make_async_copy(rest, upd, zlsem.at[0, 2])
-    count = sum(name in ("a", "o") for name, _ in HEAD)
-    run(HEAD[:count])
+    run(HEAD[:3])
     local_starts()
-    run(HEAD[count:])
+    run(HEAD[3:])
     rest_copy.wait()
 
     @pl.loop(0, NG - 1)
@@ -360,6 +390,7 @@
             sem((4,)),
             sem((2, 3)),
             sem((NG, 2)),
+            pltpu.SemaphoreType.REGULAR,
         ],
         compiler_params=pltpu.CompilerParams(
             collective_id=0, has_side_effects=True, vmem_limit_bytes=24 * 1024 * 1024

time: 61.4 us -> 57.6 us (0.938)
  Pallas kernels: 60.6 us -> 56.8 us
    pallas_call x1, Pallas kernels: 58.6 us -> 54.8 us  [per_device(): pl.pallas_call(kernel, out_shape=(pltpu.VMEM((64, 256), f32), pltpu.VMEM(...]
where the time goes in v3:
time: 57.6 us; the launch traced here: 57.5 us
  Pallas kernels  56.8 us (99%)
  between operations  0.64 us (1%)
    pallas_call x1, Pallas kernels, per_device(): pl.pallas_call(kernel, out_shape=(pltpu.VMEM((64, 256), f32), pltpu.VMEM(...  54.8 us
    pallas_call x1, Pallas kernels, per_device(): pl.pallas_call(finish, out_shape=(jax.ShapeDtypeStruct((64, 256), f32), j...  2.08 us

profile of v3, /device:TPU:1, one launch (start us, length us, event | category | flops | bytes accessed | tf_op | source)
XLA Modules:
  0.0 57.5 jit_solution(631934366215358343)
XLA Ops:
  0.6 54.8 %shard_map.103 = (f32[64,256]{1,0:T(8,128)S(1)}, f32[64,256]{1,0:T(8,128)S(1)}, f32[4096,256]{1,0:T(8,128)S(1)}, f32[8,2,2,4,4,16,512]{6,5,4,3,2,1,0:T(8,128)S(1)}, bf16[2,2,256,512]{3,2,1,0:T(8,128)(2,1)S(1)}) custom-call(f32[64,512]{1,0:T(8,128)} %a1.1, f32[64,512]{1,0:T(8,128)} %a2.1, f32[64,512]{1,0:T(8,128)} %cp.1, f32[16,4096]{1,0:T(8,128)} %bitcast.2, ...), custom_call_target="tpu_custom_call" | custom-call | tf_op jit(solution)/shard_map/pallas_call | solution.py:369
  55.4 2.1 %shard_map.104 = (f32[64,256]{1,0:T(8,128)}, f32[64,256]{1,0:T(8,128)}, f32[4096,256]{1,0:T(8,128)}) custom-call(f32[64,256]{1,0:T(8,128)S(1)} %get-tuple-element.8.out1, f32[64,256]{1,0:T(8,128)S(1)} %get-tuple-element.9.out2, f32[4096,256]{1,0:T(8,128)S(1)} %get-tuple-element.10.upd, f32[8,2,2,4,4,16,512]{6,5,4,3,2,1,0:T(8,128)S(1)} %get-tuple-element.11.grid, ...), custom_call_target="tpu_custom_call" | custom-call | tf_op jit(solution)/shard_map/pallas_call | solution.py:413

commit v4 on v3

--- a/solution.py
+++ b/solution.py
@@ -10,18 +10,18 @@
 MESH = pl.DeviceIdType.MESH
 NG = 8
 HEAD = (
-    ("a", 0), ("a", 1), ("o", 0), ("a", 2), ("a", 3), ("o", 1),
-    ("a", 4), ("b", 0), ("a", 5), ("b", 1), ("b", 2), ("a", 6),
-    ("z0", 1), ("z1", 1), ("a", 7), ("c", 0), ("b", 3), ("b", 4),
-    ("c", 1), ("z0", 2), ("c", 2), ("b", 5), ("z1", 2), ("b", 6),
-    ("b", 7), ("z0", 3), ("c", 3), ("d", 0), ("c", 4), ("d", 1),
-    ("z1", 3), ("c", 5), ("c", 6), ("d", 2), ("l", 0), ("c", 7),
-    ("d", 3), ("l", 1), ("d", 4), ("e", 0), ("d", 5), ("s", 0),
-    ("e", 1), ("s", 1), ("d", 6),
+    ("a", 0), ("a", 1), ("a", 2), ("a", 3), ("a", 4), ("a", 5),
+    ("o", 0), ("o", 1), ("b", 0), ("b", 1), ("a", 6), ("z0", 1),
+    ("b", 2), ("z1", 1), ("b", 3), ("b", 4), ("z0", 2), ("c", 0),
+    ("a", 7), ("c", 1), ("b", 5), ("b", 6), ("z1", 2), ("c", 2),
+    ("z0", 3), ("b", 7), ("c", 3), ("c", 4), ("d", 0), ("d", 1),
+    ("z1", 3), ("c", 5), ("c", 6), ("d", 2), ("c", 7), ("l", 0),
+    ("d", 3), ("d", 4), ("l", 1), ("s", 0), ("e", 0), ("e", 1),
+    ("d", 5), ("d", 6), ("s", 1), ("e", 2),
 )
 TAIL = (
     (),
-    (("e", 2), ("d", 7),),
+    (("d", 7),),
     (("e", 3),),
     (("e", 4),),
     (("e", 5),),

time: 57.6 us -> 57 us (0.990)
  no operation moved by 1% of the time
where the time goes in v4:
time: 57 us
  Pallas kernels  56.3 us (99%)
  between operations  0.64 us (1%)
    pallas_call x1, Pallas kernels, per_device(): pl.pallas_call(kernel, out_shape=(pltpu.VMEM((64, 256), f32), pltpu.VMEM(...  54.2 us
    pallas_call x1, Pallas kernels, per_device(): pl.pallas_call(finish, out_shape=(jax.ShapeDtypeStruct((64, 256), f32), j...  2.08 us

profile of v4, /device:TPU:1, one launch (start us, length us, event | category | flops | bytes accessed | tf_op | source)
XLA Modules:
  0.0 57.0 jit_solution(15773247287421151570)
XLA Ops:
  0.6 54.2 %shard_map.103 = (f32[64,256]{1,0:T(8,128)S(1)}, f32[64,256]{1,0:T(8,128)S(1)}, f32[4096,256]{1,0:T(8,128)S(1)}, f32[8,2,2,4,4,16,512]{6,5,4,3,2,1,0:T(8,128)S(1)}, bf16[2,2,256,512]{3,2,1,0:T(8,128)(2,1)S(1)}) custom-call(f32[64,512]{1,0:T(8,128)} %a1.1, f32[64,512]{1,0:T(8,128)} %a2.1, f32[64,512]{1,0:T(8,128)} %cp.1, f32[16,4096]{1,0:T(8,128)} %bitcast.2, ...), custom_call_target="tpu_custom_call" | custom-call | tf_op jit(solution)/shard_map/pallas_call | solution.py:369
  54.9 2.1 %shard_map.104 = (f32[64,256]{1,0:T(8,128)}, f32[64,256]{1,0:T(8,128)}, f32[4096,256]{1,0:T(8,128)}) custom-call(f32[64,256]{1,0:T(8,128)S(1)} %get-tuple-element.8.out1, f32[64,256]{1,0:T(8,128)S(1)} %get-tuple-element.9.out2, f32[4096,256]{1,0:T(8,128)S(1)} %get-tuple-element.10.upd, f32[8,2,2,4,4,16,512]{6,5,4,3,2,1,0:T(8,128)S(1)} %get-tuple-element.11.grid, ...), custom_call_target="tpu_custom_call" | custom-call | tf_op jit(solution)/shard_map/pallas_call | solution.py:413

commit v5 on v4

--- a/solution.py
+++ b/solution.py
@@ -9,6 +9,7 @@
 
 MESH = pl.DeviceIdType.MESH
 NG = 8
+LATE = 2
 HEAD = (
     ("a", 0), ("a", 1), ("a", 2), ("a", 3), ("a", 4), ("a", 5),
     ("o", 0), ("o", 1), ("b", 0), ("b", 1), ("a", 6), ("z0", 1),
@@ -149,12 +150,17 @@
         for p in range(2):
             pt, a, b, ap, am, bp, bm = panels[p]
             s = ssem.at[g, p]
-            for k, db, to, half in ((3, 3, bp, 0), (4, 1, bm, 2)):
+            for k, db, to in ((3, 3, bp), (4, 1, bm)):
                 bi = (b + db) % 4
                 ref = grid.at[g, p, h, bi]
                 take(ref, rsem.at[g, p, k])
-                part = grid.at[g, p, h, bi, pl.ds(half, 2)]
-                send(part, part, s, rsem.at[g, p, 5], to)
+                less, more = ((3, 2), (0, 1))[k - 3]
+                sizes = ((1, b == less), (3, b == more), (2, (b != less) & (b != more)))
+                for size, mine in sizes if g >= NG - LATE else ((2, None),):
+                    at = 0 if k == 3 else 4 - size
+                    part = grid.at[g, p, h, bi, pl.ds(at, size)]
+                    go = functools.partial(send, part, part, s, rsem.at[g, p, 5], to)
+                    go() if mine is None else pl.when(mine)(go)
                 send(ref, ref, bsem.at[g, p], rsem.at[g, p, 6], sib)
 
     def stage_e(g):
@@ -338,11 +344,24 @@
     for p in range(2):
         take(grid.at[NG - 1, p, oh], rsem.at[NG - 1, p, 6])
 
+    def sent(g, p, chunks):
+        take(upd.at[pl.ds(0, chunks * rows // 16)], ssem.at[g, p])
+
     @pl.loop(0, NG)
     def _(g):
         for p in range(2):
-            take(upd.at[pl.ds(0, 15 * rows // 16)], ssem.at[g, p])
             take(grid.at[g, p, h], bsem.at[g, p])
+
+    @pl.loop(0, NG - LATE)
+    def _(g):
+        for p in range(2):
+            sent(g, p, 15)
+
+    for g in range(NG - LATE, NG):
+        for p, b in enumerate((y, x)):
+            inner = (b == 1) | (b == 2)
+            pl.when(inner)(functools.partial(sent, g, p, 16))
+            pl.when(jnp.logical_not(inner))(functools.partial(sent, g, p, 14))
 
     take(zb1.at[pl.ds(0, 7)], zssem.at[0])
     take(zb2.at[pl.ds(0, 7)], zssem.at[1])

time: 57 us -> 57.1 us (level)
  no operation moved by 1% of the time
where the time goes in v5:
time: 57.1 us; the launch traced here: 57 us
  Pallas kernels  56.4 us (99%)
  between operations  0.64 us (1%)
    pallas_call x1, Pallas kernels, per_device(): pl.pallas_call(kernel, out_shape=(pltpu.VMEM((64, 256), f32), pltpu.VMEM(...  54.3 us
    pallas_call x1, Pallas kernels, per_device(): pl.pallas_call(finish, out_shape=(jax.ShapeDtypeStruct((64, 256), f32), j...  2.08 us

profile of v5, /device:TPU:1, one launch (start us, length us, event | category | flops | bytes accessed | tf_op | source)
XLA Modules:
  0.0 57.0 jit_solution(12731543209731983534)
XLA Ops:
  0.6 54.3 %shard_map.103 = (f32[64,256]{1,0:T(8,128)S(1)}, f32[64,256]{1,0:T(8,128)S(1)}, f32[4096,256]{1,0:T(8,128)S(1)}, f32[8,2,2,4,4,16,512]{6,5,4,3,2,1,0:T(8,128)S(1)}, bf16[2,2,256,512]{3,2,1,0:T(8,128)(2,1)S(1)}) custom-call(f32[64,512]{1,0:T(8,128)} %a1.1, f32[64,512]{1,0:T(8,128)} %a2.1, f32[64,512]{1,0:T(8,128)} %cp.1, f32[16,4096]{1,0:T(8,128)} %bitcast.2, ...), custom_call_target="tpu_custom_call" | custom-call | tf_op jit(solution)/shard_map/pallas_call | solution.py:388
  55.0 2.1 %shard_map.104 = (f32[64,256]{1,0:T(8,128)}, f32[64,256]{1,0:T(8,128)}, f32[4096,256]{1,0:T(8,128)}) custom-call(f32[64,256]{1,0:T(8,128)S(1)} %get-tuple-element.8.out1, f32[64,256]{1,0:T(8,128)S(1)} %get-tuple-element.9.out2, f32[4096,256]{1,0:T(8,128)S(1)} %get-tuple-element.10.upd, f32[8,2,2,4,4,16,512]{6,5,4,3,2,1,0:T(8,128)S(1)} %get-tuple-element.11.grid, ...), custom_call_target="tpu_custom_call" | custom-call | tf_op jit(solution)/shard_map/pallas_call | solution.py:432
